TPU v7x, 32 devices: a whole 2x2x4 slice. The times are simulated.
32 devices in a mesh: role: 2 (over core), wide: 4 (over y, x), tp: 4 (over z).
Axes of the slice: x: 2, y: 2, z: 4, core: 2. Of those that a mesh axis runs over, the one named last changes fastest.
Arguments:
- normed: bfloat16 [2048, 4096], P('wide', ('role', 'tp')), may hold values from -0.29882812 to 0.29882812
- queries: bfloat16 [2048, 4096], P('wide', 'tp'), may hold values from -4 to 4
- keys: bfloat16 [2048, 1024], P('wide'), may hold values from -4 to 4
- values: bfloat16 [2048, 1024], P('wide'), may hold values from -6 to 6
- attn_out: bfloat16 [2048, 4096], P('wide', 'tp'), may hold values from -0.29882812 to 0.29882812
- row_logsumexp: float32 [32, 2048], P('tp'), as said below
- out_grad: bfloat16 [2048, 4096], P('wide', ('role', 'tp')), may hold values from -6 to 6
- out_weight: bfloat16 [4096, 4096], P('tp'), may hold values from -0.09375 to 0.09375
- qkv_weight: bfloat16 [4096, 6144], P(('role', 'tp')), may hold values from -0.09375 to 0.09375
- documents: int32 [2048], replicated, may hold values from 0 to 2, as said below
- tasks: int32 [4, 8, 2], replicated, may hold values from -1 to 7, as said below
Outputs:
- normed_grad: bfloat16 [2048, 4096], P('wide', ('role', 'tp'))
- out_weight_grad: bfloat16 [4096, 4096], P('tp', ('role', 'wide'))
- qkv_weight_grad: bfloat16 [4096, 6144], P(('role', 'tp'), 'wide')
Inputs may be any that keep to these rules, and one draw needn't show every extreme that they name: `documents`: document numbers never fall along the tokens, and every number from 0 to 2 is used. `tasks`: row s lists in its first slots the query blocks of server s, in [s, j, 0], followed by slots holding -1 in both places; every query block from 0 to 7 stands in exactly one slot of the table; [s, j, 1] is the block holding the first token of the document of the query block's first token. row_logsumexp[h, i] is the logarithm of the sum, over the tokens j that token i may attend, of exp(scores[h, i, j]) as computed from queries and keys.
All inputs are finite; a program needn't handle non-finite values.
Results may differ from a plain program's by a relative error of at most 0.018.
Values may be sent and summed in bfloat16 or wider, within the bound.
No kernel may reach another device: no remote copies, remote signals or barrier semaphores. Data moves between devices by JAX's collectives and lax.ppermute only.
A program may use at most 128 MiB of HBM per device.

v0:
```python
import jax
import jax.numpy as jnp
from jax import lax
from jax.sharding import PartitionSpec as P

D = 4096
QUERY_HEADS = 32
KEY_VALUE_HEADS = 8
HEAD_SIZE = 128


def local(
    normed,
    queries,
    keys,
    values,
    attn_out,
    row_logsumexp,
    out_grad,
    out_weight,
    qkv_weight,
    documents,
    tasks,
):
    role_pos = lax.axis_index("role")
    is_worker = role_pos == 0
    wide_count = lax.axis_size("wide")
    wide_pos = lax.axis_index("wide")
    tp_pos = lax.axis_index("tp")
    local_rows = normed.shape[0]
    row_halves = local_rows // 2
    head_count = queries.shape[1] // HEAD_SIZE
    pair_count = head_count // 2
    kv_count = max(1, head_count // 4)
    score_scale = HEAD_SIZE ** (-0.5)
    total_rows = wide_count * local_rows
    block_count = tasks.shape[1]
    full_grad = lax.all_gather(out_grad, ("role", "tp"), axis=1, tiled=True)
    grad_half = lax.dynamic_slice_in_dim(full_grad, role_pos * (D // 2), D // 2, 1)
    out_part = lax.dot_general(
        attn_out, grad_half, (((0,), (0,)), ((), ())), preferred_element_type=jnp.float32
    )

    def worker_side():
        return lax.dot_general(
            full_grad, out_weight, (((1,), (1,)), ((), ())), preferred_element_type=jnp.float32
        ).astype(jnp.bfloat16)

    def server_side():
        return queries

    first_piece = lax.cond(is_worker, worker_side, server_side)
    kv_start = tp_pos * head_count // 4 * HEAD_SIZE
    key_cols = lax.dynamic_slice_in_dim(keys, kv_start, kv_count * HEAD_SIZE, 1)
    value_cols = lax.dynamic_slice_in_dim(values, kv_start, kv_count * HEAD_SIZE, 1)
    kv_piece = jnp.where(is_worker, key_cols, value_cols)
    out_piece = lax.dynamic_slice_in_dim(
        attn_out, role_pos * pair_count * HEAD_SIZE, pair_count * HEAD_SIZE, 1
    )
    gathered = (
        lax.all_gather(first_piece, ("role", "wide"), axis=0, tiled=True),
        lax.all_gather(kv_piece, ("role", "wide"), axis=0, tiled=True),
        lax.all_gather(out_piece, ("role", "wide"), axis=0, tiled=True),
    )
    grad_all = gathered[0][:total_rows]
    query_all = gathered[0][total_rows:]
    key_all = gathered[1][:total_rows]
    value_all = gathered[1][total_rows:]
    output_all = gathered[2].reshape(2, total_rows, pair_count, HEAD_SIZE)
    delta_all = jnp.einsum(
        "irpd,ripd->rpi",
        grad_all.reshape(total_rows, 2, pair_count, HEAD_SIZE),
        output_all,
        preferred_element_type=jnp.float32,
    ).reshape(pair_count, 2, total_rows)
    lse_all = row_logsumexp.reshape(pair_count, 2, total_rows)

    def tile(block_q, block_k, query_grad, kv_acc):
        offsets = jnp.arange(row_halves, dtype=jnp.int32)
        query_pos = block_q * row_halves + offsets
        key_pos = block_k * row_halves + offsets
        query_rows = lax.dynamic_slice_in_dim(
            query_all, block_q * row_halves, row_halves, 0
        ).reshape(row_halves, pair_count, 2, HEAD_SIZE)
        grad_rows = lax.dynamic_slice_in_dim(grad_all, block_q * row_halves, row_halves, 0).reshape(
            row_halves, pair_count, 2, HEAD_SIZE
        )
        key_rows = lax.dynamic_slice_in_dim(key_all, block_k * row_halves, row_halves, 0).reshape(
            row_halves, kv_count, HEAD_SIZE
        )
        value_rows = lax.dynamic_slice_in_dim(
            value_all, block_k * row_halves, row_halves, 0
        ).reshape(row_halves, kv_count, HEAD_SIZE)
        if head_count >= 4:
            key_rows = jnp.repeat(key_rows, 2, axis=1)
            value_rows = jnp.repeat(value_rows, 2, axis=1)
        lse_rows = lax.dynamic_slice_in_dim(lse_all, block_q * row_halves, row_halves, 2)
        delta_rows = lax.dynamic_slice_in_dim(delta_all, block_q * row_halves, row_halves, 2)
        query_docs = lax.dynamic_slice_in_dim(documents, block_q * row_halves, row_halves, 0)
        key_docs = lax.dynamic_slice_in_dim(documents, block_k * row_halves, row_halves, 0)
        allowed = (query_docs[:, None] == key_docs[None, :]) & (
            key_pos[None, :] <= query_pos[:, None]
        )
        scores = (
            jnp.einsum("qphd,cpd->phqc", query_rows, key_rows, preferred_element_type=jnp.float32)
            * score_scale
        )
        probs = jnp.exp(jnp.where(allowed, scores - lse_rows[..., None], -jnp.inf))
        probs_low = probs.astype(jnp.bfloat16)
        value_grad = jnp.einsum(
            "phqc,qphd->cpd", probs_low, grad_rows, preferred_element_type=jnp.float32
        )
        prob_grad = jnp.einsum(
            "qphd,cpd->phqc", grad_rows, value_rows, preferred_element_type=jnp.float32
        )
        score_grad = (probs * (prob_grad - delta_rows[..., None]) * score_scale).astype(
            jnp.bfloat16
        )
        query_tile = jnp.einsum(
            "phqc,cpd->qphd", score_grad, key_rows, preferred_element_type=jnp.float32
        )
        query_grad = query_grad + query_tile.reshape(row_halves, head_count * HEAD_SIZE)
        key_grad = jnp.einsum(
            "phqc,qphd->cpd", score_grad, query_rows, preferred_element_type=jnp.float32
        )
        tile_kv = jnp.concatenate([key_grad, value_grad], axis=2).reshape(
            row_halves, pair_count * 2 * HEAD_SIZE
        )
        target = block_k % 2 * wide_count + block_k // 2
        current = lax.dynamic_index_in_dim(kv_acc, target, 0, keepdims=False)
        kv_acc = lax.dynamic_update_index_in_dim(kv_acc, current + tile_kv, target, 0)
        return (query_grad, kv_acc)

    def empty_side():
        return (
            jnp.zeros((block_count, row_halves, head_count * HEAD_SIZE), jnp.float32),
            jnp.zeros((block_count, row_halves, pair_count * 2 * HEAD_SIZE), jnp.float32),
        )

    def attend_side():
        own_row = lax.dynamic_index_in_dim(tasks, wide_pos, 0, keepdims=False)

        def slot_turn(number, carry):
            query_acc, kv_acc = carry
            block_q = own_row[number, 0]
            valid = block_q >= 0
            safe_q = jnp.maximum(block_q, 0)
            upper = jnp.where(valid, safe_q + 1, 0)
            lower = jnp.where(valid, own_row[number, 1], 0)

            def key_turn(block_k, inner):
                return tile(safe_q, block_k, inner[0], inner[1])

            start = jnp.zeros((row_halves, head_count * HEAD_SIZE), jnp.float32)
            query_grad, kv_acc = lax.fori_loop(lower, upper, key_turn, (start, kv_acc))
            target = safe_q % 2 * wide_count + safe_q // 2
            current = lax.dynamic_index_in_dim(query_acc, target, 0, keepdims=False)
            query_acc = lax.dynamic_update_index_in_dim(query_acc, current + query_grad, target, 0)
            return (query_acc, kv_acc)

        return lax.fori_loop(0, block_count, slot_turn, empty_side())

    query_acc, kv_acc = lax.cond(is_worker, empty_side, attend_side)
    kv_flat = kv_acc.reshape(block_count * row_halves, pair_count * 2 * HEAD_SIZE)
    kv_sum = lax.psum_scatter(
        kv_flat.astype(jnp.bfloat16), ("role", "wide"), scatter_dimension=0, tiled=True
    )
    arrived = lax.all_to_all(
        query_acc.astype(jnp.bfloat16), ("role", "wide"), split_axis=0, concat_axis=0, tiled=True
    )
    query_piece = jnp.sum(arrived.astype(jnp.float32), axis=0).astype(jnp.bfloat16)
    head_q, key_value_head = (
        lax.all_gather(query_piece, ("role", "tp"), axis=1, tiled=True),
        lax.all_gather(kv_sum, ("role", "tp"), axis=1, tiled=True),
    )
    query_grads = head_q.reshape(row_halves, 2, QUERY_HEADS * HEAD_SIZE)
    grouped_queries = jnp.sum(
        key_value_head.reshape(row_halves, 2, KEY_VALUE_HEADS, 2, 2 * HEAD_SIZE).astype(
            jnp.float32
        ),
        axis=3,
    ).astype(jnp.bfloat16)
    key_gradients = grouped_queries[..., :HEAD_SIZE].reshape(
        row_halves, 2, KEY_VALUE_HEADS * HEAD_SIZE
    )
    value_gradients = grouped_queries[..., HEAD_SIZE:].reshape(
        row_halves, 2, KEY_VALUE_HEADS * HEAD_SIZE
    )
    qkv_grads = jnp.concatenate([query_grads, key_gradients, value_gradients], axis=2)
    normed_grad = jnp.einsum(
        "irc,nc->rin", qkv_grads, qkv_weight, preferred_element_type=jnp.float32
    )
    normed_grad = normed_grad.reshape(local_rows, qkv_weight.shape[0]).astype(jnp.bfloat16)
    qkv_part = jnp.einsum(
        "rin,irc->nc",
        normed.reshape(2, row_halves, normed.shape[1]),
        qkv_grads,
        preferred_element_type=jnp.float32,
    )
    out_sum, qkv_sum = (
        lax.psum_scatter(
            out_part.astype(jnp.bfloat16), "wide", scatter_dimension=1, tiled=True
        ).astype(jnp.float32),
        lax.psum_scatter(
            qkv_part.astype(jnp.bfloat16), "wide", scatter_dimension=1, tiled=True
        ).astype(jnp.float32),
    )
    return (normed_grad, out_sum.astype(jnp.bfloat16), qkv_sum.astype(jnp.bfloat16))


def solution(mesh):
    in_specs = (
        P("wide", ("role", "tp")),
        P("wide", "tp"),
        P("wide", None),
        P("wide", None),
        P("wide", "tp"),
        P("tp", None),
        P("wide", ("role", "tp")),
        P("tp", None),
        P(("role", "tp"), None),
        P(),
        P(),
    )
    out_specs = (P("wide", ("role", "tp")), P("tp", ("role", "wide")), P(("role", "tp"), "wide"))
    return jax.shard_map(local, mesh=mesh, in_specs=in_specs, out_specs=out_specs, check_vma=False)
```

profile of v0, /device:TPU:0, one launch (start us, length us, event | category | flops | bytes accessed | tf_op | source)
XLA Modules:
  0.0 686.1 jit_solution(5662846886879194408)
XLA Ops:
  9.6 49.6 %all-gather.7.cloned.1.call-done = bf16[512,4096]{1,0:T(8,128)(2,1)} async-done(((bf16[512,512]{1,0:T(8,128)(2,1)}), bf16[512,4096]{1,0:T(8,128)(2,1)}) %all-gather.7.cloned.1.call-update) | async-done | bytes 4194320 | tf_op jit(solution)/shard_map/all_gather | solution.py:38
  59.2 9.2 %conditional.2 = (bf16[512,1024]{1,0:T(8,128)(2,1)S(1)}) conditional(s32[]{:T(128)} %convert_element_type.57, (bf16[512,1024]{1,0:T(8,128)(2,1)S(1)}) %tuple.68, (bf16[512,4096]{1,0:T(8,128)(2,1)}, bf16[1024,4096]{1,0:T(8,128)(2,1)}) %tuple.64), branch_computations={%region_0.0_spmd, %region_1.0_spmd} | conditional | flops 4295491584 | bytes 13631496 | solution.py:52
  59.2 9.2 %convolution_convert_fusion = bf16[512,1024]{1,0:T(8,128)(2,1)S(1)} fusion(bf16[512,4096]{1,0:T(8,128)(2,1)} %get-tuple-element.517, bf16[1024,4096]{1,0:T(8,128)(2,1)} %get-tuple-element.570), kind=kOutput, calls=%fused_computation | convolution fusion | flops 4295491584 | bytes 13631488 | tf_op jit(solution)/shard_map/cond/branch_1_fun/dot_general | solution.py:45
  72.0 25.1 %all-gather.11.cloned.1.call-done = bf16[4096,512]{1,0:T(8,128)(2,1)} async-done(((bf16[512,512]{1,0:T(8,128)(2,1)}), bf16[4096,512]{1,0:T(8,128)(2,1)}) %all-gather.11.cloned.1.call-update) | async-done | bytes 4194320 | tf_op jit(solution)/shard_map/all_gather | solution.py:63
  97.1 6.9 %reshape.119 = bf16[2,2048,4,128]{3,2,1,0:T(4,128)(2,1)} reshape(bf16[4096,512]{1,0:T(8,128)(2,1)} %all-gather.11.cloned.1.call-done) | data formatting | bytes 8388608 | tf_op jit(solution)/shard_map/reshape | solution.py:69
  104.0 6.3 bitcast_convert_fusion.1
  110.3 45.1 %all-gather.9.cloned.1.call-done = bf16[4096,1024]{0,1:T(8,128)(2,1)} async-done(((bf16[512,1024]{0,1:T(8,128)(2,1)}), bf16[4096,1024]{0,1:T(8,128)(2,1)}) %all-gather.9.cloned.1.call-update) | async-done | bytes 8388624 | tf_op jit(solution)/shard_map/all_gather | solution.py:61
  155.4 2.5 slice.30
  158.0 2.0 copy-done.1
  159.9 4.3 convert.2
  164.2 21.7 %all-gather.13.cloned.1.call-done = bf16[4096,256]{0,1:T(8,128)(2,1)} async-done(((bf16[512,256]{0,1:T(8,128)(2,1)}), bf16[4096,256]{0,1:T(8,128)(2,1)}) %all-gather.13.cloned.1.call-update) | async-done | bytes 2097168 | tf_op jit(solution)/shard_map/all_gather | solution.py:62
  185.9 7.9 %conditional.3 = (f32[8,256,1024]{1,2,0:T(8,128)}, f32[8,256,1024]{1,2,0:T(8,128)}) conditional(s32[]{:T(128)} %convert_element_type.57, (s32[]{:T(128)}, s32[4,8,2]{1,2,0:T(2,128)}, s32[2048]{0:T(1024)}, bf16[4096,1024]{0,1:T(8,128)(2,1)}, f32[8,2048]{1,0:T(8,128)S(1)}, /*index=5*/bf16[2048,1024]{0,1:T(8,128)(2,1)}, ...), branch_computations={%region_2.7_spmd.clone, %region_7.8_spmd} | conditional | flops 680706560 | bytes 96333480 | solution.py:163
  185.9 4.0 broadcast.49.clone
  189.9 4.0 broadcast.49
  193.8 7.3 %copy.57 = bf16[8,256,1024]{2,1,0:T(8,128)(2,1)} copy(f32[8,256,1024]{1,2,0:T(8,128)} %get-tuple-element.565) | data formatting | bytes 12582912 | tf_op jit(solution)/shard_map/cond | solution.py:163
  201.1 3.8 convert_element_type.58
  205.0 240.8 %all_to_all.5 = bf16[8,256,1024]{1,2,0:T(8,128)(2,1)} all-to-all(bf16[8,256,1024]{1,2,0:T(8,128)(2,1)S(1)} %convert_element_type.58), channel_id=1, replica_groups=mesh['role'=2,'wide'=4,'tp'=4] {'role','wide'}, dimensions={0} | all-to-all | bytes 8388608 | tf_op jit(solution)/shard_map/all_to_all | solution.py:168
  445.8 3.7 reduce_sum.24
  449.6 3.7 reduce-scatter.4.cloned.1.call-done
  453.4 6.0 convert_bitcast_fusion
  459.7 42.5 %all-gather.15.cloned.1.call-done = bf16[256,8192]{0,1:T(8,128)(2,1)} async-done(((bf16[256,1024]{0,1:T(8,128)(2,1)}), bf16[256,8192]{0,1:T(8,128)(2,1)}) %all-gather.15.cloned.1.call-update) | async-done | bytes 4194320 | tf_op jit(solution)/shard_map/all_gather | solution.py:173
  502.2 6.3 copy.60
  508.6 41.0 %all-gather.17.cloned.1.call-done = bf16[256,8192]{1,0:T(8,128)(2,1)} async-done(((bf16[256,1024]{1,0:T(8,128)(2,1)}), bf16[256,8192]{1,0:T(8,128)(2,1)}) %all-gather.17.cloned.1.call-update) | async-done | bytes 4194320 | tf_op jit(solution)/shard_map/all_gather | solution.py:174
  549.5 7.8 %reshape.122 = bf16[256,2,8,2,256]{4,3,2,1,0:T(2,128)(2,1)} reshape(bf16[256,8192]{1,0:T(8,128)(2,1)} %all-gather.17.cloned.1.call-done) | data formatting | bytes 8388608 | tf_op jit(solution)/shard_map/reshape | solution.py:178
  557.3 11.6 %reduce_sum.25 = bf16[256,2,8,256]{3,2,1,0:T(8,128)(2,1)S(1)} reduce(bf16[256,2,8,2,256]{4,3,2,1,0:T(2,128)(2,1)} %reshape.122, bf16[]{:T(256)} %constant.263.clone.1), dimensions={3}, to_apply=%region_10.11 | reduce | flops 1048576 | bytes 6291458 | tf_op jit(solution)/shard_map/reduce_sum | solution.py:177
  568.9 1.7 fusion.16
  574.9 8.5 %fusion.6 = bf16[512,6144]{0,1:T(8,128)(2,1)} fusion(bf16[2,256,512]{2,1,0:T(8,128)(2,1)} %bitcast.171, bf16[256,2,1024]{2,0,1:T(8,128)(2,1)S(1)} %copy.85, bf16[256,2,1024]{2,0,1:T(8,128)(2,1)S(1)} %copy.84, bf16[256,2,4096]{2,0,1:T(8,128)(2,1)} %copy.60), kind=kOutput, calls=%fused_computation.32 | convolution fusion | flops 3243245568 | bytes 13107200 | tf_op jit(solution)/shard_map/rin,irc->nc/dot_general | solution.py:194
  583.5 20.5 %reduce-scatter.6.cloned.1.call-done = bf16[1024,512]{0,1:T(8,128)(2,1)} async-done(((bf16[1024,2048]{0,1:T(8,128)(2,1)}), bf16[1024,512]{0,1:T(8,128)(2,1)}) %reduce-scatter.6.cloned.1.call-update) | async-done | bytes 1048592 | tf_op jit(solution)/shard_map/reduce_scatter | solution.py:201
  603.9 2.3 copy.62
  606.2 8.3 %fusion.10 = bf16[256,2,512]{2,0,1:T(8,128)(2,1)} fusion(bf16[512,6144]{1,0:T(8,128)(2,1)} %param.27, bf16[256,2,1024]{2,0,1:T(8,128)(2,1)S(1)} %copy-done.3, bf16[256,2,1024]{2,0,1:T(8,128)(2,1)S(1)} %copy.84, bf16[256,2,4096]{2,0,1:T(8,128)(2,1)} %copy.60), kind=kOutput, calls=%fused_computation.39 | convolution fusion | flops 3240361984 | bytes 13107200 | tf_op jit(solution)/shard_map/irc,nc->rin/dot_general | solution.py:190
  614.5 62.5 %reduce-scatter.8.cloned.1.call-done = bf16[512,1536]{0,1:T(8,128)(2,1)} async-done(((bf16[512,6144]{0,1:T(8,128)(2,1)}), bf16[512,1536]{0,1:T(8,128)(2,1)}) %reduce-scatter.8.cloned.1.call-update) | async-done | bytes 1572880 | tf_op jit(solution)/shard_map/reduce_scatter | solution.py:204
  677.0 2.6 copy.63
  (38 shorter events, 10.7 us)
Async XLA Ops:
  7.2 1.5 copy-start
  7.2 52.0 %all-gather.7.cloned.1.call-start = ((), (), s32[]{:S(2)}) async-start(), calls=%async_computation.4 | async-start | bytes 4718592 | tf_op jit(solution)/shard_map/all_gather | solution.py:38
  8.6 88.5 %all-gather.11.cloned.1.call-start = ((), (), s32[]{:S(2)}) async-start(), calls=%async_computation.6 | async-start | bytes 4718592 | tf_op jit(solution)/shard_map/all_gather | solution.py:63
  9.6 145.9 %all-gather.9.cloned.1.call-start = ((), (), s32[]{:S(2)}) async-start(), calls=%async_computation.5 | async-start | bytes 9437184 | tf_op jit(solution)/shard_map/all_gather | solution.py:61
  69.7 116.1 %all-gather.13.cloned.1.call-start = ((), (), s32[]{:S(2)}) async-start(), calls=%async_computation.7 | async-start | bytes 2359296 | tf_op jit(solution)/shard_map/all_gather | solution.py:62
  71.9 381.4 %reduce-scatter.4.cloned.1.call-start = ((), (), s32[]{:S(2)}) async-start(), calls=%async_computation.9 | async-start | bytes 4718592 | tf_op jit(solution)/shard_map/reduce_scatter | solution.py:165
  157.9 2.0 copy-start.1
  159.9 26.0 %copy-start.4 = (f32[8,2048]{1,0:T(8,128)S(1)}, f32[8,2048]{1,0:T(8,128)}, u32[]{:S(2)}) copy-start(f32[8,2048]{1,0:T(8,128)} %param.24) | copy-start | bytes 196612
  201.1 301.1 %all-gather.15.cloned.1.call-start = ((), (), s32[]{:S(2)}) async-start(), calls=%async_computation.8 | async-start | bytes 4718592 | tf_op jit(solution)/shard_map/all_gather | solution.py:173
  449.5 100.0 %all-gather.17.cloned.1.call-start = ((), (), s32[]{:S(2)}) async-start(), calls=%async_computation.10 | async-start | bytes 4718592 | tf_op jit(solution)/shard_map/all_gather | solution.py:174
  453.3 150.6 %reduce-scatter.6.cloned.1.call-start = ((), (), s32[]{:S(2)}) async-start(), calls=%async_computation.11 | async-start | bytes 5242880 | tf_op jit(solution)/shard_map/reduce_scatter | solution.py:201
  459.5 217.6 %reduce-scatter.8.cloned.1.call-start = ((), (), s32[]{:S(2)}) async-start(), calls=%async_computation.12 | async-start | bytes 7864320 | tf_op jit(solution)/shard_map/reduce_scatter | solution.py:204
  574.0 1.0 copy-start.2
  583.4 22.8 %copy-start.3 = (bf16[256,2,1024]{2,0,1:T(8,128)(2,1)S(1)}, bf16[256,2,1024]{2,0,1:T(8,128)(2,1)}, u32[]{:S(2)}) copy-start(bf16[256,2,1024]{2,0,1:T(8,128)(2,1)} %copy-done.2) | copy-start | bytes 3145732
Sparse Core Ops, SparseCore 0:
  9.6 49.5 all-gather.6
  61.7 35.3 all-gather.10
  99.5 55.8 all-gather.8
  157.8 28.0 all-gather.12
  201.2 252.0 reduce-scatter.3
  455.3 46.8 all-gather.14
  503.8 45.6 all-gather.16
  552.5 51.3 reduce-scatter.5
  606.9 70.0 reduce-scatter.7
where the time goes:
time: 690 us; the launch traced here: 686 us
  waiting for transfers between devices  312 us (45%)
  blocking collectives  241 us (35%)
  local copies, waits for them, and re-layouts  56.4 us (8%)
  matrix products  32 us (5%)
  other arithmetic  30.5 us (4%)
  between operations  14 us (2%)
    all_to_all x1, blocking collectives, local(): lax.all_to_all(query_acc.astype(jnp.bfloat16), ('role', 'wide'), split_ax...  241 us
    reduce_scatter x1, waiting for transfers between devices, local(): lax.psum_scatter(qkv_part.astype(jnp.bfloat16), 'wide', scatter_dimension...  62.5 us
    all_gather x1, waiting for transfers between devices, local(): full_grad = lax.all_gather(out_grad, ('role', 'tp'), axis=1, tiled=True)  49.6 us
    all_gather x1, waiting for transfers between devices, local(): lax.all_gather(first_piece, ('role', 'wide'), axis=0, tiled=True)  45.1 us
    all_gather x1, waiting for transfers between devices, local(): lax.all_gather(query_piece, ('role', 'tp'), axis=1, tiled=True)  42.5 us
    all_gather x1, waiting for transfers between devices, local(): lax.all_gather(kv_sum, ('role', 'tp'), axis=1, tiled=True)  41 us
    all_gather x1, waiting for transfers between devices, local(): lax.all_gather(out_piece, ('role', 'wide'), axis=0, tiled=True)  25.1 us
    all_gather x1, waiting for transfers between devices, local(): lax.all_gather(kv_piece, ('role', 'wide'), axis=0, tiled=True)  21.7 us
  transfers between devices with their start and end apart: 9, of which 9 were waited for; matrix products, arithmetic and copies ran while one was open for 14% of the time, Pallas kernels for 0%

commit v1 on v0

--- a/solution.py
+++ b/solution.py
@@ -7,6 +7,25 @@
 QUERY_HEADS = 32
 KEY_VALUE_HEADS = 8
 HEAD_SIZE = 128
+
+
+def lay_desk_on(inner_x, which_dim):
+    e_next = list(inner_x.shape[1:])
+    e_next[which_dim] *= inner_x.shape[0]
+    return jnp.moveaxis(inner_x, 0, which_dim).reshape(e_next)
+
+
+def wait_face(array_in, mesh_name):
+    shares = lax.axis_size(mesh_name)
+    opened = array_in[None]
+    for ii in range(shares.bit_length() - 1):
+        f_next = 1 << ii
+        mid_arr = lax.ppermute(opened, mesh_name, [(pp, pp ^ f_next) for pp in range(shares)])
+        top = jnp.stack([opened, mid_arr], 0)
+        ready = lax.axis_index(mesh_name)
+        response = ready >> ii & 1
+        opened = jnp.where(response == 0, top, top[::-1]).reshape(-1, *array_in.shape)
+    return opened
 
 
 def local(
@@ -35,7 +54,8 @@
     score_scale = HEAD_SIZE ** (-0.5)
     total_rows = wide_count * local_rows
     block_count = tasks.shape[1]
-    full_grad = lax.all_gather(out_grad, ("role", "tp"), axis=1, tiled=True)
+    placed = wait_face(out_grad, ("role", "tp"))
+    full_grad = lay_desk_on(placed, 1)
     grad_half = lax.dynamic_slice_in_dim(full_grad, role_pos * (D // 2), D // 2, 1)
     out_part = lax.dot_general(
         attn_out, grad_half, (((0,), (0,)), ((), ())), preferred_element_type=jnp.float32

time: 690 us -> 663 us (0.961)
  waiting for transfers between devices: 312 us -> 269 us
    ppermute x0 -> x3, waiting for transfers between devices: none -> 61.4 us  [wait_face(): lax.ppermute(opened, mesh_name, [(pp, pp ^ f_next) for pp in range(shares)])]
    all_gather x1 -> x0, waiting for transfers between devices: 49.6 us -> none  [local(): full_grad = lax.all_gather(out_grad, ('role', 'tp'), axis=1, tiled=True)]
    all_gather x1, waiting for transfers between devices: 25.1 us -> 0.02 us  [local(): lax.all_gather(out_piece, ('role', 'wide'), axis=0, tiled=True)]
    reduce_scatter x1, waiting for transfers between devices: 20.5 us -> 0.03 us  [local(): lax.psum_scatter(out_part.astype(jnp.bfloat16), 'wide', scatter_dimension...]
  transfers between devices with their start and end apart: 9 -> 11, of which waited for: 9 -> 9; matrix products, arithmetic and copies ran while one was open for 14% -> 16% of each run, Pallas kernels for 0% -> 0%
where the time goes in v1:
time: 663 us; the launch traced here: 659 us
  waiting for transfers between devices  269 us (41%)
  blocking collectives  240 us (36%)
  local copies, waits for them, and re-layouts  57.9 us (9%)
  other arithmetic  36.4 us (5%)
  matrix products  33.2 us (5%)
  between operations  15.8 us (2%)
    all_to_all x1, blocking collectives, local(): lax.all_to_all(query_acc.astype(jnp.bfloat16), ('role', 'wide'), split_ax...  240 us
    ppermute x3, waiting for transfers between devices, wait_face(): lax.ppermute(opened, mesh_name, [(pp, pp ^ f_next) for pp in range(shares)])  61.4 us
    reduce_scatter x1, waiting for transfers between devices, local(): lax.psum_scatter(qkv_part.astype(jnp.bfloat16), 'wide', scatter_dimension...  57.2 us
    all_gather x1, waiting for transfers between devices, local(): lax.all_gather(query_piece, ('role', 'tp'), axis=1, tiled=True)  42.5 us
    all_gather x1, waiting for transfers between devices, local(): lax.all_gather(first_piece, ('role', 'wide'), axis=0, tiled=True)  41.7 us
    all_gather x1, waiting for transfers between devices, local(): lax.all_gather(kv_sum, ('role', 'tp'), axis=1, tiled=True)  40.7 us
    all_gather x1, waiting for transfers between devices, local(): lax.all_gather(kv_piece, ('role', 'wide'), axis=0, tiled=True)  21.8 us
  transfers between devices with their start and end apart: 11, of which 9 were waited for; matrix products, arithmetic and copies ran while one was open for 16% of the time, Pallas kernels for 0%

profile of v1, /device:TPU:0, one launch (start us, length us, event | category | flops | bytes accessed | tf_op | source)
XLA Modules:
  0.0 658.8 jit_solution(8647721238110526426)
XLA Ops:
  10.1 3.1 collective-permute-start
  13.2 12.1 %collective-permute-done = bf16[1,512,512]{2,1,0:T(8,128)(2,1)S(1)} collective-permute-done((bf16[1,512,512]{2,1,0:T(8,128)(2,1)}, bf16[1,512,512]{2,1,0:T(8,128)(2,1)S(1)}, u32[]{:S(2)}, u32[]{:S(2)}) %collective-permute-start) | collective-permute-done | bytes 524320 | tf_op jit(solution)/shard_map/ppermute | solution.py:23
  26.8 2.8 collective-permute-start.1
  29.6 45.0 %collective-permute-done.1 = bf16[2,512,512]{2,1,0:T(8,128)(2,1)} collective-permute-done((bf16[2,512,512]{2,1,0:T(8,128)(2,1)S(1)}, bf16[2,512,512]{2,1,0:T(8,128)(2,1)}, u32[]{:S(2)}, u32[]{:S(2)}) %collective-permute-start.1) | collective-permute-done | bytes 1048608 | tf_op jit(solution)/shard_map/ppermute | solution.py:23
  76.6 4.3 collective-permute-done.2
  83.8 2.6 copy.96
  86.3 9.2 %conditional.2 = (bf16[512,1024]{1,0:T(8,128)(2,1)S(1)}) conditional(s32[]{:T(128)} %convert_element_type.57, (bf16[512,1024]{1,0:T(8,128)(2,1)S(1)}) %tuple.144, (bf16[512,4096]{1,0:T(8,128)(2,1)}, bf16[1024,4096]{1,0:T(8,128)(2,1)}) %tuple.143), branch_computations={%region_0.1_spmd, %region_1.2_spmd} | conditional | flops 4295491584 | bytes 13631496 | solution.py:72
  86.3 9.2 %convolution_convert_fusion = bf16[512,1024]{1,0:T(8,128)(2,1)S(1)} fusion(bf16[512,4096]{1,0:T(8,128)(2,1)} %get-tuple-element.517, bf16[1024,4096]{1,0:T(8,128)(2,1)} %get-tuple-element.570), kind=kOutput, calls=%fused_computation | convolution fusion | flops 4295491584 | bytes 13631488 | tf_op jit(solution)/shard_map/cond/branch_1_fun/dot_general | solution.py:65
  99.2 7.0 %reshape.135 = bf16[2,2048,4,128]{3,2,1,0:T(4,128)(2,1)} reshape(bf16[4096,512]{1,0:T(8,128)(2,1)} %all-gather.8.cloned.1.call-done) | data formatting | bytes 8388608 | tf_op jit(solution)/shard_map/reshape | solution.py:89
  106.2 6.2 bitcast_convert_fusion.1
  112.4 41.7 %all-gather.6.cloned.1.call-done = bf16[4096,1024]{0,1:T(8,128)(2,1)} async-done(((bf16[512,1024]{0,1:T(8,128)(2,1)}), bf16[4096,1024]{0,1:T(8,128)(2,1)}) %all-gather.6.cloned.1.call-update) | async-done | bytes 8388624 | tf_op jit(solution)/shard_map/all_gather | solution.py:81
  154.0 2.5 slice.30
  158.5 4.3 convert.2
  162.8 21.8 %all-gather.10.cloned.1.call-done = bf16[4096,256]{0,1:T(8,128)(2,1)} async-done(((bf16[512,256]{0,1:T(8,128)(2,1)}), bf16[4096,256]{0,1:T(8,128)(2,1)}) %all-gather.10.cloned.1.call-update) | async-done | bytes 2097168 | tf_op jit(solution)/shard_map/all_gather | solution.py:82
  184.6 7.9 %conditional.3 = (f32[8,256,1024]{1,2,0:T(8,128)}, f32[8,256,1024]{1,2,0:T(8,128)}) conditional(s32[]{:T(128)} %convert_element_type.57, (s32[]{:T(128)}, s32[4,8,2]{1,2,0:T(2,128)}, s32[2048]{0:T(1024)}, bf16[4096,1024]{0,1:T(8,128)(2,1)}, f32[8,2048]{1,0:T(8,128)S(1)}, /*index=5*/bf16[2048,1024]{0,1:T(8,128)(2,1)}, ...), branch_computations={%region_2.7_spmd.clone, %region_7.8_spmd} | conditional | flops 680706560 | bytes 96333480 | solution.py:183
  184.6 4.0 broadcast.49.clone
  188.6 4.0 broadcast.49
  192.5 7.3 %copy.60 = bf16[8,256,1024]{2,1,0:T(8,128)(2,1)} copy(f32[8,256,1024]{1,2,0:T(8,128)} %get-tuple-element.565) | data formatting | bytes 12582912 | tf_op jit(solution)/shard_map/cond | solution.py:183
  199.9 3.8 convert_element_type.58
  203.7 239.7 %all_to_all.5 = bf16[8,256,1024]{1,2,0:T(8,128)(2,1)} all-to-all(bf16[8,256,1024]{1,2,0:T(8,128)(2,1)S(1)} %convert_element_type.58), channel_id=1, replica_groups=mesh['role'=2,'wide'=4,'tp'=4] {'role','wide'}, dimensions={0} | all-to-all | bytes 8388608 | tf_op jit(solution)/shard_map/all_to_all | solution.py:188
  443.4 3.7 reduce_sum.24
  447.2 3.7 reduce-scatter.4.cloned.1.call-done
  451.0 6.0 convert_bitcast_fusion
  457.3 42.5 %all-gather.12.cloned.1.call-done = bf16[256,8192]{0,1:T(8,128)(2,1)} async-done(((bf16[256,1024]{0,1:T(8,128)(2,1)}), bf16[256,8192]{0,1:T(8,128)(2,1)}) %all-gather.12.cloned.1.call-update) | async-done | bytes 4194320 | tf_op jit(solution)/shard_map/all_gather | solution.py:193
  499.8 6.4 copy.63
  506.3 40.7 %all-gather.14.cloned.1.call-done = bf16[256,8192]{1,0:T(8,128)(2,1)} async-done(((bf16[256,1024]{1,0:T(8,128)(2,1)}), bf16[256,8192]{1,0:T(8,128)(2,1)}) %all-gather.14.cloned.1.call-update) | async-done | bytes 4194320 | tf_op jit(solution)/shard_map/all_gather | solution.py:194
  547.0 7.8 %reshape.138 = bf16[256,2,8,2,256]{4,3,2,1,0:T(2,128)(2,1)} reshape(bf16[256,8192]{1,0:T(8,128)(2,1)} %all-gather.14.cloned.1.call-done) | data formatting | bytes 8388608 | tf_op jit(solution)/shard_map/reshape | solution.py:198
  554.8 11.4 %reduce_sum.25 = bf16[256,2,8,256]{3,2,1,0:T(8,128)(2,1)S(1)} reduce(bf16[256,2,8,2,256]{4,3,2,1,0:T(2,128)(2,1)} %reshape.138, bf16[]{:T(256)} %constant.266.clone.1), dimensions={3}, to_apply=%region_10.11 | reduce | flops 1048576 | bytes 6291458 | tf_op jit(solution)/shard_map/reduce_sum | solution.py:197
  571.2 8.7 %fusion.6 = bf16[512,6144]{0,1:T(8,128)(2,1)} fusion(bf16[2,256,512]{2,1,0:T(8,128)(2,1)} %bitcast.196, bf16[256,2,1024]{2,0,1:T(8,128)(2,1)S(1)} %copy.89, bf16[256,2,1024]{2,0,1:T(8,128)(2,1)} %copy.88, bf16[256,2,4096]{2,0,1:T(8,128)(2,1)} %copy.63), kind=kOutput, calls=%fused_computation.32 | convolution fusion | flops 3243245568 | bytes 13107200 | tf_op jit(solution)/shard_map/rin,irc->nc/dot_general | solution.py:214
  582.3 9.3 %fusion.10 = bf16[256,2,512]{2,0,1:T(8,128)(2,1)} fusion(bf16[512,6144]{1,0:T(8,128)(2,1)} %param.27, bf16[256,2,1024]{2,0,1:T(8,128)(2,1)S(1)} %copy.89, bf16[256,2,1024]{2,0,1:T(8,128)(2,1)S(1)} %copy-done.4, bf16[256,2,4096]{2,0,1:T(8,128)(2,1)} %copy.63), kind=kOutput, calls=%fused_computation.44 | convolution fusion | flops 3240361984 | bytes 13107200 | tf_op jit(solution)/shard_map/irc,nc->rin/dot_general | solution.py:210
  591.6 57.2 %reduce-scatter.8.cloned.1.call-done = bf16[512,1536]{0,1:T(8,128)(2,1)} async-done(((bf16[512,6144]{0,1:T(8,128)(2,1)}), bf16[512,1536]{0,1:T(8,128)(2,1)}) %reduce-scatter.8.cloned.1.call-update) | async-done | bytes 1572880 | tf_op jit(solution)/shard_map/reduce_scatter | solution.py:224
  648.8 2.6 copy.66
  (49 shorter events, 21.6 us)
Async XLA Ops:
  8.0 1.2 copy-start
  8.0 91.1 %all-gather.8.cloned.1.call-start = ((), (), s32[]{:S(2)}) async-start(), calls=%async_computation.5 | async-start | bytes 4718592 | tf_op jit(solution)/shard_map/all_gather | solution.py:83
  10.1 143.9 %all-gather.6.cloned.1.call-start = ((), (), s32[]{:S(2)}) async-start(), calls=%async_computation.4 | async-start | bytes 9437184 | tf_op jit(solution)/shard_map/all_gather | solution.py:81
  10.1 15.3 %collective-permute-start = (bf16[1,512,512]{2,1,0:T(8,128)(2,1)}, bf16[1,512,512]{2,1,0:T(8,128)(2,1)S(1)}, u32[]{:S(2)}, u32[]{:S(2)}) collective-permute-start(bf16[1,512,512]{2,1,0:T(8,128)(2,1)} %bitcast.193), channel_id=1, source_target_pairs={{0,1},{1,0},{2,3},{3,2},{16,17},{17,16},{18,19},{19,18},{4,5},{5,4... | collective-permute-start | bytes 1572872 | tf_op jit(solution)/shard_map/ppermute | solution.py:23
  26.8 47.9 %collective-permute-start.1 = (bf16[2,512,512]{2,1,0:T(8,128)(2,1)S(1)}, bf16[2,512,512]{2,1,0:T(8,128)(2,1)}, u32[]{:S(2)}, u32[]{:S(2)}) collective-permute-start(bf16[2,512,512]{2,1,0:T(8,128)(2,1)S(1)} %get-tuple-element.689), channel_id=1, source_target_pairs={{0,2},{1,3},{2,0},{3,1},{16,18},{17,19},{18,16},{19,17},{4,6},{5,7... | collective-permute-start | bytes 3145736 | tf_op jit(solution)/shard_map/ppermute | solution.py:23
  76.5 4.4 collective-permute-start.2
  83.8 2.6 copy-start.2
  96.9 87.7 %all-gather.10.cloned.1.call-start = ((), (), s32[]{:S(2)}) async-start(), calls=%async_computation.6 | async-start | bytes 2359296 | tf_op jit(solution)/shard_map/all_gather | solution.py:82
  99.1 351.9 %reduce-scatter.4.cloned.1.call-start = ((), (), s32[]{:S(2)}) async-start(), calls=%async_computation.8 | async-start | bytes 4718592 | tf_op jit(solution)/shard_map/reduce_scatter | solution.py:185
  156.5 2.0 copy-start.1
  158.5 26.1 %copy-start.5 = (f32[8,2048]{1,0:T(8,128)S(1)}, f32[8,2048]{1,0:T(8,128)}, u32[]{:S(2)}) copy-start(f32[8,2048]{1,0:T(8,128)} %param.24) | copy-start | bytes 196612
  199.8 300.0 %all-gather.12.cloned.1.call-start = ((), (), s32[]{:S(2)}) async-start(), calls=%async_computation.7 | async-start | bytes 4718592 | tf_op jit(solution)/shard_map/all_gather | solution.py:193
  447.1 99.9 %all-gather.14.cloned.1.call-start = ((), (), s32[]{:S(2)}) async-start(), calls=%async_computation.9 | async-start | bytes 4718592 | tf_op jit(solution)/shard_map/all_gather | solution.py:194
  451.0 129.0 %reduce-scatter.6.cloned.1.call-start = ((), (), s32[]{:S(2)}) async-start(), calls=%async_computation.10 | async-start | bytes 5242880 | tf_op jit(solution)/shard_map/reduce_scatter | solution.py:221
  457.1 191.7 %reduce-scatter.8.cloned.1.call-start = ((), (), s32[]{:S(2)}) async-start(), calls=%async_computation.11 | async-start | bytes 7864320 | tf_op jit(solution)/shard_map/reduce_scatter | solution.py:224
  567.9 2.7 copy-start.3
  579.9 2.4 copy-start.4
Sparse Core Ops, SparseCore 0:
  11.3 39.2 all-gather.7
  97.0 56.9 all-gather.5
  156.5 28.0 all-gather.9
  199.9 250.9 reduce-scatter.3
  452.9 46.8 all-gather.11
  501.3 45.6 all-gather.13
Sparse Core Ops, SparseCore 1:
  457.1 52.5 reduce-scatter.5
  580.0 68.7 reduce-scatter.7
